TPU v7x, 256 devices: a whole 4x4x8 slice. The times are simulated.
256 devices in a mesh: span: 16 (over z, x_hi), sp: 8 (over y, x_lo), fsdp: 2 (over core).
Axes of the slice: x: 4 (x_hi: 2, x_lo: 2; x = x_hi * 2 + x_lo), y: 4, z: 8, core: 2. Of those that a mesh axis runs over, the one named last changes fastest.
Arguments:
- query_pre: bfloat16 [2, 16384, 3072], P('fsdp', ('span', 'sp')), may hold values from -12 to 12
- key_pre: bfloat16 [2, 16384, 3072], P('fsdp', ('span', 'sp')), may hold values from -12 to 12
- values: bfloat16 [2, 16384, 3072], P('fsdp', ('span', 'sp')), may hold values from -6 to 6
- cotangent: bfloat16 [2, 16384, 3072], P('fsdp', ('span', 'sp')), may hold values from -6 to 6
- gains: float32 [2, 3072], P(None, 'fsdp'), may hold values from 0.5 to 1.5
- frame_span: int32 [2, 16384], P('fsdp', 'span'), may hold values from 0 to 31, as said below
- denoise_steps: int32 [2, 32], P('fsdp'), may hold values from 1 to 4
Outputs:
- query_grad: bfloat16 [2, 16384, 3072], P('fsdp', ('span', 'sp'))
- key_grad: bfloat16 [2, 16384, 3072], P('fsdp', ('span', 'sp'))
- value_grad: bfloat16 [2, 16384, 3072], P('fsdp', ('span', 'sp'))
- gain_grad: float32 [2, 3072], P(None, 'fsdp')
Inputs may be any that keep to these rules, and one draw needn't show every extreme that they name: `frame_span`: never falls along a video. Group g (tokens g * 1024 to (g + 1) * 1024 - 1) holds frame spans 2 g and 2 g + 1, each from a quarter to three quarters of the group's tokens.
All inputs are finite; a program needn't handle non-finite values.
Results may differ from a plain program's by a relative error of at most 0.0081.
The roundings to bfloat16 on the way count: a program that leaves them out, or rounds other values in their place, can miss the bound.
Values may be sent and summed in bfloat16 or wider, within the bound.
No kernel may reach another device: no remote copies, remote signals or barrier semaphores. Data moves between devices by JAX's collectives and lax.ppermute only.
A program may use at most 128 MiB of HBM per device.

v0:
```python
import jax
import jax.numpy as jnp
from jax import lax
from jax.sharding import PartitionSpec as P

HDIM = 128
EPSILON = 1e-06
NEGATIVE = -1e30


def from_behind(value, axis, steps):
    count = lax.axis_size(axis)
    first, last = (max(0, -steps), min(count, count - steps))
    return lax.ppermute(value, axis, [(source, source + steps) for source in range(first, last)])


def normed(raw_rows, gain_row):
    wide = raw_rows.astype(jnp.float32)
    inverse_rms = lax.rsqrt(jnp.mean(wide * wide, axis=-1, keepdims=True) + EPSILON)
    normal_rows = wide * inverse_rms
    return (normal_rows, inverse_rms, (normal_rows * gain_row).astype(jnp.bfloat16))


def norm_backward(grad_rows, normal_rows, inverse_rms, gain_row):
    upstream = grad_rows.astype(jnp.float32)
    scaled = upstream * gain_row
    inner = jnp.mean(scaled * normal_rows, axis=-1, keepdims=True)
    result = (inverse_rms * (scaled - normal_rows * inner)).astype(jnp.bfloat16)
    return (result, jnp.sum(upstream * normal_rows, axis=0))


def across(left, right):
    return lax.dot_general(
        left, right, (((1,), (1,)), ((), ())), preferred_element_type=jnp.float32
    )


def downward(left, right):
    return lax.dot_general(
        left, right, (((0,), (0,)), ((), ())), preferred_element_type=jnp.float32
    )


def head_grads(
    query_head, grad_head, key_joined, value_joined, joined_mask, step_weight, own_width
):
    score_scale = HDIM ** (-0.5)
    scores = across(query_head, key_joined) * score_scale
    masked = jnp.where(joined_mask, scores, NEGATIVE)
    row_max = jnp.max(masked, axis=1)
    row_total = jnp.sum(jnp.exp(masked - row_max[:, None]), axis=1)
    log_total = row_max + jnp.log(row_total)
    grad_prob = across(grad_head, value_joined)
    probs = jnp.where(joined_mask, jnp.exp(scores - log_total[:, None]), 0.0)
    row_delta = jnp.sum(probs * grad_prob, axis=1)
    factor = step_weight[:, None]
    sgrad = (factor * probs * (grad_prob - row_delta[:, None])).astype(jnp.bfloat16)
    weights = (factor * probs).astype(jnp.bfloat16)
    query_part = jnp.dot(sgrad, key_joined, preferred_element_type=jnp.float32) * score_scale
    key_own_grad = downward(sgrad[:, :own_width], query_head) * score_scale
    value_own_grad = downward(weights[:, :own_width], grad_head)
    return (
        query_part,
        key_own_grad,
        value_own_grad,
        sgrad[:, own_width:],
        weights[:, own_width:],
        log_total,
        row_delta,
    )


def on_device(query_pre, key_pre, values, cotangent, gains, frame_span, denoise_steps):
    gain_full = lax.all_gather(gains, "fsdp", axis=1, tiled=True)
    q_normal, q_inverse, q_ready = normed(query_pre[0], gain_full[0])
    k_normal, k_inverse, k_ready = normed(key_pre[0], gain_full[1])
    heads_query, heads_key, heads_value, heads_grad = (
        lax.all_to_all(q_ready, "sp", split_axis=1, concat_axis=0, tiled=True),
        lax.all_to_all(k_ready, "sp", split_axis=1, concat_axis=0, tiled=True),
        lax.all_to_all(values[0], "sp", split_axis=1, concat_axis=0, tiled=True),
        lax.all_to_all(cotangent[0], "sp", split_axis=1, concat_axis=0, tiled=True),
    )
    head_count = heads_query.shape[1] // HDIM
    own_width = heads_query.shape[0]
    span_ids = frame_span[0]
    step_table = denoise_steps[0].astype(jnp.float32)
    matches = span_ids[:, None] == lax.iota(jnp.int32, step_table.shape[0])[None, :]
    step_weight = jnp.sum(jnp.where(matches, step_table[None, :], 0.0), axis=1)
    group_index = lax.axis_index("span")
    key_prev, value_prev = from_behind((heads_key, heads_value), "span", 1)
    own_mask = span_ids[None, :] <= span_ids[:, None]
    prev_open = group_index > 0
    prev_mask = jnp.broadcast_to(prev_open, own_mask.shape)
    joined_mask = jnp.concatenate([own_mask, prev_mask], axis=1)
    key_joined_all = jnp.concatenate([heads_key, key_prev], axis=0)
    value_joined_all = jnp.concatenate([heads_value, value_prev], axis=0)
    query_parts = []
    key_parts = []
    value_parts = []
    sgrad_list = []
    weight_list = []
    total_list = []
    delta_list = []
    for head_index in range(head_count):
        first = head_index * HDIM
        last = first + HDIM
        outcome = head_grads(
            heads_query[:, first:last],
            heads_grad[:, first:last],
            key_joined_all[:, first:last],
            value_joined_all[:, first:last],
            joined_mask,
            step_weight,
            own_width,
        )
        query_parts.append(outcome[0])
        key_parts.append(outcome[1])
        value_parts.append(outcome[2])
        sgrad_list.append(outcome[3])
        weight_list.append(outcome[4])
        total_list.append(outcome[5])
        delta_list.append(outcome[6])
    query_attn = jnp.concatenate(query_parts, axis=1)
    key_own = jnp.concatenate(key_parts, axis=1)
    value_own = jnp.concatenate(value_parts, axis=1)
    key_terms = []
    value_terms = []
    for head_index in range(head_count):
        first = head_index * HDIM
        last = first + HDIM
        key_terms.append(
            downward(sgrad_list[head_index], heads_query[:, first:last]) * HDIM ** (-0.5)
        )
        value_terms.append(downward(weight_list[head_index], heads_grad[:, first:last]))
    key_back, value_back = from_behind(
        (jnp.concatenate(key_terms, axis=1), jnp.concatenate(value_terms, axis=1)), "span", -1
    )
    key_attn = key_own + key_back
    value_attn = value_own + value_back
    query_tokens, key_tokens, value_tokens = (
        lax.all_to_all(
            query_attn.astype(jnp.bfloat16), "sp", split_axis=0, concat_axis=1, tiled=True
        ),
        lax.all_to_all(
            key_attn.astype(jnp.bfloat16), "sp", split_axis=0, concat_axis=1, tiled=True
        ),
        lax.all_to_all(
            value_attn.astype(jnp.bfloat16), "sp", split_axis=0, concat_axis=1, tiled=True
        ),
    )
    query_back, query_gain = norm_backward(query_tokens, q_normal, q_inverse, gain_full[0])
    key_back_rows, key_gain = norm_backward(key_tokens, k_normal, k_inverse, gain_full[1])
    partial_value = jnp.stack([query_gain, key_gain])
    summed = lax.psum(partial_value, ("span", "sp"))
    gain_grad = lax.psum_scatter(summed, "fsdp", scatter_dimension=1, tiled=True)
    return (query_back[None], key_back_rows[None], value_tokens[None], gain_grad)


def solution(mesh):
    placed = (
        P("fsdp", ("span", "sp"), None),
        P("fsdp", ("span", "sp"), None),
        P("fsdp", ("span", "sp"), None),
        P("fsdp", ("span", "sp"), None),
        P(None, "fsdp"),
        P("fsdp", "span"),
        P("fsdp", None),
    )
    return jax.shard_map(
        on_device,
        mesh=mesh,
        in_specs=placed,
        out_specs=(
            P("fsdp", ("span", "sp"), None),
            P("fsdp", ("span", "sp"), None),
            P("fsdp", ("span", "sp"), None),
            P(None, "fsdp"),
        ),
        check_vma=False,
    )
```

profile of v0, /device:TPU:0, one launch (start us, length us, event | category | flops | bytes accessed | tf_op | source)
XLA Modules:
  0.0 1031.0 jit_solution(12937883028764885410)
XLA Ops:
  9.5 4.2 all-to-all-start.2
  18.8 7.4 all-to-all-done.2
  26.2 3.5 all-to-all-start.1
  32.1 9.4 all-to-all-done.1
  41.5 4.3 all-to-all-start.3
  46.3 5.9 collective-permute-start
  53.5 6.6 all-to-all-done.3
  60.1 4.2 all-to-all-start
  69.7 2.9 collective-permute-start.1
  72.6 12.8 %all-to-all-done = bf16[128,8,384]{2,0,1:T(8,128)(2,1)} async-done(((bf16[128,8,384]{2,0,1:T(8,128)(2,1)}), bf16[128,8,384]{2,0,1:T(8,128)(2,1)}, u32[]{:S(2)}, u32[]{:S(2)}) %all-to-all-start) | async-done | bytes 786464 | tf_op jit(solution)/shard_map/all_to_all | solution.py:78
  90.4 9.0 fusion.9
  99.4 8.6 exponential_reduce_fusion.2
  108.0 5.4 fusion.68
  113.4 5.4 fusion.61
  118.9 20.2 %fusion.6 = (f32[1024]{0:T(1024)S(1)}, f32[1024]{0:T(1024)S(1)}, f32[1024]{0:T(1024)S(1)}, f32[2048,1024]{0,1:T(8,128)}) fusion(f32[1024]{0:T(1024)S(1)} %log_add_fusion.2, f32[1024,2048]{1,0:T(8,128)} %get-tuple-element.37, pred[1024,1024]{1,0:T(32,128)(4,1)S(1)} %broadcast_compare_fusion, pred[]{:T(512)S(6)} %gt.3, f32[2048,1024]{0,1:T(8,128)} %fusion.68, ...), kind=kOutput, calls=%fused_computation.18 | convolution fusion | flops 569373696 | bytes 53239808 | tf_op jit(solution)/shard_map/dot_general | solution.py:33
  139.1 12.5 %multiply_convert_fusion.2 = (bf16[1024,2048]{1,0:T(8,128)(2,1)S(1)}, bf16[1024,2048]{1,0:T(8,128)(2,1)S(1)}, bf16[1024,2048]{1,0:T(8,128)(2,1)S(1)}, bf16[1024,2048]{1,0:T(8,128)(2,1)S(1)}) fusion(f32[1024]{0:T(1024)S(1)} %select_reduce_fusion, f32[1024]{0:T(1024)S(1)} %log_add_fusion.2, f32[1024,2048]{1,0:T(8,128)} %get-tuple-element.37, ...), kind=kLoop, calls=%fused_computation.26 | loop fusion | flops 33554432 | bytes 51400704 | tf_op jit(solution)/shard_map/convert_element_type | solution.py:58
  159.8 3.3 fusion.38
  168.2 4.9 multiply_convert_fusion.1
  173.1 3.2 fusion.50
  176.2 3.5 fusion.56
  185.2 4.3 all-to-all-start.4
  189.6 2.8 pad_maximum_fusion
  211.6 21.7 %collective-permute-done.2 = f32[1024,384]{1,0:T(8,128)} collective-permute-done((f32[1024,384]{1,0:T(8,128)}, f32[1024,384]{1,0:T(8,128)}, u32[]{:S(2)}, u32[]{:S(2)}) %collective-permute-start.2) | collective-permute-done | bytes 1572896 | tf_op jit(solution)/shard_map/ppermute | solution.py:14
  235.9 5.6 all-to-all-start.5
  241.5 2.7 multiply_convert_fusion.4
  244.2 19.0 %collective-permute-done.3 = f32[1024,384]{0,1:T(8,128)} collective-permute-done((f32[1024,384]{0,1:T(8,128)}, f32[1024,384]{0,1:T(8,128)}, u32[]{:S(2)}, u32[]{:S(2)}) %collective-permute-start.3) | collective-permute-done | bytes 1572896 | tf_op jit(solution)/shard_map/ppermute | solution.py:14
  263.2 2.9 copy_bitcast_fusion
  266.1 10.1 all-to-all-done.5
  276.2 4.2 all-to-all-start.6
  288.2 5.7 all-to-all-done.6
  296.2 37.5 %reduce-scatter.4.cloned.1.call-done = f32[1536,2]{1,0:T(8,128)} async-done(((f32[3072,2]{1,0:T(8,128)}), f32[1536,2]{1,0:T(8,128)}) %reduce-scatter.4.cloned.1.call-update) | async-done | bytes 12304
  335.0 688.9 %psum.8 = f32[2,1536]{1,0:T(2,128)} all-reduce(f32[2,1536]{1,0:T(2,128)S(1)} %copy.105), channel_id=1, replica_groups=mesh['span'=16,'sp'=8,'fsdp'=2] {'span','sp'}, use_global_device_ids=true, to_apply=%region_16.17 | all-reduce | flops 3072 | bytes 24576 | tf_op jit(solution)/shard_map/psum | solution.py:154
  (114 shorter events, 73.6 us)
Async XLA Ops:
  7.2 10.0 copy-start.7
  9.5 16.7 %all-to-all-start.2 = ((bf16[128,8,384]{0,2,1:T(8,128)(2,1)}), bf16[128,8,384]{0,2,1:T(8,128)(2,1)}, u32[]{:S(2)}, u32[]{:S(2)}) async-start(bf16[128,8,384]{0,2,1:T(8,128)(2,1)} %bitcast.7), calls=%async_computation.2 | async-start | bytes 1572864 | tf_op jit(solution)/shard_map/all_to_all | solution.py:80
  17.2 28.6 %copy-start.5 = (bf16[1,128,3072]{2,1,0:T(8,128)(2,1)S(1)}, bf16[1,128,3072]{2,1,0:T(8,128)(2,1)}, u32[]{:S(2)}) copy-start(bf16[1,128,3072]{2,1,0:T(8,128)(2,1)} %param.7) | copy-start | bytes 2359300
  26.2 15.2 %all-to-all-start.1 = ((bf16[128,8,384]{2,0,1:T(8,128)(2,1)}), bf16[128,8,384]{2,0,1:T(8,128)(2,1)S(1)}, u32[]{:S(2)}, u32[]{:S(2)}) async-start(bf16[128,8,384]{2,0,1:T(8,128)(2,1)} %multiply_convert_fusion.5), calls=%async_computation.1 | async-start | bytes 1572864 | tf_op jit(solution)/shard_map/all_to_all | solution.py:79
  41.5 22.9 %copy-start.20 = (s32[1,32]{1,0:T(1,128)S(1)}, s32[1,32]{1,0:T(1,128)}, u32[]{:S(2)}) copy-start(s32[1,32]{1,0:T(1,128)} %param.13) | copy-start | bytes 388
  41.5 22.9 %copy-start.19 = (s32[1,1024]{1,0:T(1,128)S(1)}, s32[1,1024]{1,0:T(1,128)}, u32[]{:S(2)}) copy-start(s32[1,1024]{1,0:T(1,128)} %param.12) | copy-start | bytes 12292
  41.5 18.7 %all-to-all-start.3 = ((bf16[128,8,384]{0,2,1:T(8,128)(2,1)}), bf16[128,8,384]{0,2,1:T(8,128)(2,1)}, u32[]{:S(2)}, u32[]{:S(2)}) async-start(bf16[128,8,384]{0,2,1:T(8,128)(2,1)} %bitcast.118), calls=%async_computation.3 | async-start | bytes 1572864 | tf_op jit(solution)/shard_map/all_to_all | solution.py:81
  46.3 39.1 %collective-permute-start = (bf16[1024,384]{1,0:T(8,128)(2,1)S(1)}, bf16[1024,384]{1,0:T(8,128)(2,1)}, u32[]{:S(2)}, u32[]{:S(2)}) collective-permute-start(bf16[1024,384]{1,0:T(8,128)(2,1)S(1)} %bitcast.91), channel_id=1, source_target_pairs={{0,16},{16,32},{32,48},{48,64},{64,80},{80,96},{96,112},{112,128},... | collective-permute-start | bytes 2359304 | tf_op jit(solution)/shard_map/ppermute | solution.py:14
  60.1 25.3 %all-to-all-start = ((bf16[128,8,384]{2,0,1:T(8,128)(2,1)}), bf16[128,8,384]{2,0,1:T(8,128)(2,1)}, u32[]{:S(2)}, u32[]{:S(2)}) async-start(bf16[128,8,384]{2,0,1:T(8,128)(2,1)} %multiply_convert_fusion.6), calls=%async_computation | async-start | bytes 1572864 | tf_op jit(solution)/shard_map/all_to_all | solution.py:78
  69.7 38.3 %collective-permute-start.1 = (bf16[1024,384]{1,0:T(8,128)(2,1)}, bf16[1024,384]{1,0:T(8,128)(2,1)}, u32[]{:S(2)}, u32[]{:S(2)}) collective-permute-start(bf16[1024,384]{1,0:T(8,128)(2,1)} %bitcast.102), channel_id=1, source_target_pairs={{0,16},{16,32},{32,48},{48,64},{64,80},{80,96},{96,112},{112,128},... | collective-permute-start | bytes 2359304 | tf_op jit(solution)/shard_map/ppermute | solution.py:14
  87.7 11.7 %copy-start.1 = (f32[1024,2048]{1,0:T(8,128)}, f32[1024,2048]{1,0:T(8,128)S(1)}, u32[]{:S(2)}) copy-start(f32[1024,2048]{1,0:T(8,128)S(1)} %fusion.75) | copy-start | bytes 25165828
  90.4 9.0 copy-start
  99.4 8.6 copy-start.4
  99.4 8.6 copy-start.13
  139.1 12.6 %copy-start.14 = (bf16[8,128,384]{2,1,0:T(8,128)(2,1)S(1)}, bf16[8,128,384]{2,1,0:T(8,128)(2,1)}, u32[]{:S(2)}) copy-start(bf16[8,128,384]{2,1,0:T(8,128)(2,1)} %copy.81) | copy-start | bytes 2359300
  153.3 14.8 %slice-start.2 = ((s8[8388608]{0:T(1024)(128)(4,1)}), s8[4194304]{0:T(1024)(128)(4,1)S(1)}, s32[]{:S(2)}) async-start(s8[8388608]{0:T(1024)(128)(4,1)} %bitcast.89), calls=%async_computation.11 | async-start | bytes 8388608
  155.9 12.2 %slice-start = ((s8[8388608]{0:T(1024)(128)(4,1)}), s8[4194304]{0:T(1024)(128)(4,1)S(1)}, s32[]{:S(2)}) async-start(s8[8388608]{0:T(1024)(128)(4,1)} %bitcast.87), calls=%async_computation.9 | async-start | bytes 8388608
  157.2 10.9 %slice-start.3 = ((s8[8388608]{0:T(1024)(128)(4,1)}), s8[4194304]{0:T(1024)(128)(4,1)S(1)}, s32[]{:S(2)}) async-start(s8[8388608]{0:T(1024)(128)(4,1)} %bitcast.89), calls=%async_computation.12 | async-start | bytes 8388608
  159.8 8.3 slice-start.1
  185.2 10.5 %copy-start.17 = (f32[1024,128]{0,1:T(8,128)S(1)}, f32[1024,128]{0,1:T(8,128)}, u32[]{:S(2)}) copy-start(f32[1024,128]{0,1:T(8,128)} %fusion.16) | copy-start | bytes 1572868
  185.2 10.5 %copy-start.18 = (f32[1024,128]{0,1:T(8,128)S(1)}, f32[1024,128]{0,1:T(8,128)}, u32[]{:S(2)}) copy-start(f32[1024,128]{0,1:T(8,128)} %fusion.12) | copy-start | bytes 1572868
  185.2 18.3 %all-to-all-start.4 = ((bf16[8,128,384]{2,1,0:T(8,128)(2,1)}), bf16[8,128,384]{2,1,0:T(8,128)(2,1)}, u32[]{:S(2)}, u32[]{:S(2)}) async-start(bf16[8,128,384]{2,1,0:T(8,128)(2,1)} %pad_maximum_fusion.2), calls=%async_computation.4 | async-start | bytes 1572864 | tf_op jit(solution)/shard_map/all_to_all | solution.py:141
  189.6 9.2 copy-start.12
  192.4 41.0 %collective-permute-start.2 = (f32[1024,384]{1,0:T(8,128)}, f32[1024,384]{1,0:T(8,128)}, u32[]{:S(2)}, u32[]{:S(2)}) collective-permute-start(f32[1024,384]{1,0:T(8,128)} %pad_maximum_fusion), channel_id=1, source_target_pairs={{16,0},{32,16},{48,32},{64,48},{80,64},{96,80},{112,96},{128,112},... | collective-permute-start | bytes 4718600 | tf_op jit(solution)/shard_map/ppermute | solution.py:14
  197.0 6.5 copy-start.3
  197.0 66.2 %collective-permute-start.3 = (f32[1024,384]{0,1:T(8,128)}, f32[1024,384]{0,1:T(8,128)}, u32[]{:S(2)}, u32[]{:S(2)}) collective-permute-start(f32[1024,384]{0,1:T(8,128)} %pad_maximum_fusion.1), channel_id=1, source_target_pairs={{16,0},{32,16},{48,32},{64,48},{80,64},{96,80},{112,96},{128,112},... | collective-permute-start | bytes 4718600 | tf_op jit(solution)/shard_map/ppermute | solution.py:14
  205.6 27.8 %copy-start.15 = (f32[1024,128]{1,0:T(8,128)S(1)}, f32[1024,128]{1,0:T(8,128)}, u32[]{:S(2)}) copy-start(f32[1024,128]{1,0:T(8,128)} %fusion.38) | copy-start | bytes 1572868
  205.6 27.7 %copy-start.16 = (f32[1024,128]{1,0:T(8,128)S(1)}, f32[1024,128]{1,0:T(8,128)}, u32[]{:S(2)}) copy-start(f32[1024,128]{1,0:T(8,128)} %fusion.44) | copy-start | bytes 1572868
  209.0 32.5 %copy-start.6 = (bf16[1,128,3072]{2,1,0:T(8,128)(2,1)S(1)}, bf16[1,128,3072]{2,1,0:T(8,128)(2,1)}, u32[]{:S(2)}) copy-start(bf16[1,128,3072]{2,1,0:T(8,128)(2,1)} %param.7) | copy-start | bytes 2359300
  235.9 40.3 %all-to-all-start.5 = ((bf16[8,128,384]{2,1,0:T(8,128)(2,1)}), bf16[8,128,384]{2,1,0:T(8,128)(2,1)S(1)}, u32[]{:S(2)}, u32[]{:S(2)}) async-start(bf16[8,128,384]{2,1,0:T(8,128)(2,1)} %bitcast.119), calls=%async_computation.5 | async-start | bytes 1572864 | tf_op jit(solution)/shard_map/all_to_all | solution.py:144
  276.2 17.6 %all-to-all-start.6 = ((bf16[8,128,384]{1,2,0:T(8,128)(2,1)}), bf16[8,128,384]{1,2,0:T(8,128)(2,1)}, u32[]{:S(2)}, u32[]{:S(2)}) async-start(bf16[8,128,384]{1,2,0:T(8,128)(2,1)} %copy_bitcast_fusion), calls=%async_computation.6 | async-start | bytes 1572864 | tf_op jit(solution)/shard_map/all_to_all | solution.py:147
  280.5 53.2 %reduce-scatter.4.cloned.1.call-start = ((), (), s32[]{:S(2)}) async-start(), calls=%async_computation.8 | async-start | bytes 2359296
  (5 other events, 24.7 us)
Sparse Core Ops, SparseCore 0:
  287.0 46.5 reduce-scatter.3
where the time goes:
time: 1040 us; the launch traced here: 1030 us
  blocking collectives  691 us (66%)
  waiting for transfers between devices  130 us (12%)
  matrix products  79.4 us (8%)
  other arithmetic  48.8 us (5%)
  starting transfers between devices  42.3 us (4%)
  local copies, waits for them, and re-layouts  24.5 us (2%)
  between operations  14.8 us (1%)
    psum x1, blocking collectives, on_device(): summed = lax.psum(partial_value, ('span', 'sp'))  689 us
    dot_general x6, matrix products, across(): lax.dot_general(left, right, (((1,), (1,)), ((), ())), preferred_element_...  45 us
    ppermute x4, waiting for transfers between devices, from_behind(): lax.ppermute(value, axis, [(source, source + steps) for source in range(f...  40.7 us
    unnamed x2, waiting for transfers between devices  37.5 us
    dot_general x12, matrix products, downward(): lax.dot_general(left, right, (((0,), (0,)), ((), ())), preferred_element_...  26.4 us
  transfers between devices with their start and end apart: 12, of which 9 were waited for; matrix products, arithmetic and copies ran while one was open for 7% of the time, Pallas kernels for 0%

commit v1 on v0

--- a/solution.py
+++ b/solution.py
@@ -151,7 +151,7 @@
     query_back, query_gain = norm_backward(query_tokens, q_normal, q_inverse, gain_full[0])
     key_back_rows, key_gain = norm_backward(key_tokens, k_normal, k_inverse, gain_full[1])
     partial_value = jnp.stack([query_gain, key_gain])
-    summed = lax.psum(partial_value, ("span", "sp"))
+    summed = jnp.sum(lax.all_gather(partial_value, ("span", "sp")), axis=0)
     gain_grad = lax.psum_scatter(summed, "fsdp", scatter_dimension=1, tiled=True)
     return (query_back[None], key_back_rows[None], value_tokens[None], gain_grad)
 

time: 1040 us -> 962 us (0.925)
  blocking collectives: 691 us -> 2.02 us
  waiting for transfers between devices: 130 us -> 744 us
  matrix products: 79.4 us -> 67.6 us
    psum x1 -> x0, blocking collectives: 689 us -> none  [on_device(): summed = lax.psum(partial_value, ('span', 'sp'))]
    all_gather x0 -> x1, waiting for transfers between devices: none -> 628 us  [on_device(): summed = jnp.sum(lax.all_gather(partial_value, ('span', 'sp')), axis=0)]
    unnamed x2 -> x3, waiting for transfers between devices: 37.5 us -> 7.35 us
  transfers between devices with their start and end apart: 12 -> 13, of which waited for: 9 -> 10; matrix products, arithmetic and copies ran while one was open for 7% -> 8% of each run, Pallas kernels for 0% -> 0%
where the time goes in v1:
time: 962 us; the launch traced here: 953 us
  waiting for transfers between devices  744 us (77%)
  matrix products  67.6 us (7%)
  other arithmetic  55.7 us (6%)
  starting transfers between devices  39.7 us (4%)
  local copies, waits for them, and re-layouts  28.9 us (3%)
  between operations  14.9 us (2%)
    all_gather x1, waiting for transfers between devices, on_device(): summed = jnp.sum(lax.all_gather(partial_value, ('span', 'sp')), axis=0)  628 us
    ppermute x4, waiting for transfers between devices, from_behind(): lax.ppermute(value, axis, [(source, source + steps) for source in range(f...  50.4 us
    dot_general x6, matrix products, across(): lax.dot_general(left, right, (((1,), (1,)), ((), ())), preferred_element_...  43.5 us
    convert_element_type x2, other arithmetic, head_grads(): weights = (factor * probs).astype(jnp.bfloat16)  22.1 us
    dot_general x12, matrix products, downward(): lax.dot_general(left, right, (((0,), (0,)), ((), ())), preferred_element_...  20.4 us
  transfers between devices with their start and end apart: 13, of which 10 were waited for; matrix products, arithmetic and copies ran while one was open for 8% of the time, Pallas kernels for 0%

profile of v1, /device:TPU:0, one launch (start us, length us, event | category | flops | bytes accessed | tf_op | source)
XLA Modules:
  0.0 952.7 jit_solution(16917617218460601127)
XLA Ops:
  9.5 3.8 all-to-all-start.2
  19.3 7.0 all-to-all-done.2
  26.3 3.5 all-to-all-start.1
  31.0 10.9 %all-to-all-done.1 = bf16[128,8,384]{2,0,1:T(8,128)(2,1)S(1)} async-done(((bf16[128,8,384]{2,0,1:T(8,128)(2,1)}), bf16[128,8,384]{2,0,1:T(8,128)(2,1)S(1)}, u32[]{:S(2)}, u32[]{:S(2)}) %all-to-all-start.1) | async-done | bytes 786464 | tf_op jit(solution)/shard_map/all_to_all | solution.py:79
  41.8 4.3 all-to-all-start.3
  46.7 4.7 collective-permute-start
  52.7 7.8 all-to-all-done.3
  60.5 4.2 all-to-all-start
  69.7 2.5 collective-permute-start.1
  72.2 13.6 %all-to-all-done = bf16[128,8,384]{2,0,1:T(8,128)(2,1)} async-done(((bf16[128,8,384]{2,0,1:T(8,128)(2,1)}), bf16[128,8,384]{2,0,1:T(8,128)(2,1)}, u32[]{:S(2)}, u32[]{:S(2)}) %all-to-all-start) | async-done | bytes 786464 | tf_op jit(solution)/shard_map/all_to_all | solution.py:78
  88.2 2.4 fusion.82
  90.6 9.8 %fusion.9 = (f32[1024]{0:T(1024)S(1)}, f32[1024]{0:T(1024)S(1)}, f32[1024]{0:T(1024)S(1)}, f32[1024,2048]{1,0:T(8,128)}) fusion(pred[1024,1024]{1,0:T(32,128)(4,1)S(1)} %broadcast_compare_fusion, pred[]{:T(512)S(6)} %gt.3, f32[1024,2048]{1,0:T(8,128)S(1)} %fusion.82, f32[1024,2048]{1,0:T(8,128)S(1)} %fusion.75, bf16[1024,384]{1,0:T(8,128)(2,1)S(1)} %bitcast.96, ...), kind=kOutput, calls=%fused_computation.27 | convolution fusion | flops 556790784 | bytes 28061696 | tf_op jit(solution)/shard_map/dot_general | solution.py:33
  100.4 8.5 exponential_reduce_fusion.2
  109.0 5.4 fusion.68
  114.4 5.4 fusion.61
  119.8 18.1 %fusion.6 = (f32[1024]{0:T(1024)S(1)}, f32[1024]{0:T(1024)S(1)}, f32[1024]{0:T(1024)S(1)}, f32[2048,1024]{0,1:T(8,128)}) fusion(f32[1024]{0:T(1024)S(1)} %log_add_fusion.2, f32[1024,2048]{1,0:T(8,128)} %get-tuple-element.37, pred[1024,1024]{1,0:T(32,128)(4,1)S(1)} %broadcast_compare_fusion, pred[]{:T(512)S(6)} %gt.3, f32[2048,1024]{0,1:T(8,128)} %fusion.68, ...), kind=kOutput, calls=%fused_computation.18 | convolution fusion | flops 569373696 | bytes 53239808 | tf_op jit(solution)/shard_map/dot_general | solution.py:33
  137.9 10.1 %multiply_convert_fusion.1 = (bf16[1024,2048]{1,0:T(8,128)(2,1)}, bf16[1024,2048]{1,0:T(8,128)(2,1)}) fusion(f32[1024]{0:T(1024)S(1)} %select_reduce_fusion, f32[1024]{0:T(1024)S(1)} %get-tuple-element.40, f32[1024,2048]{1,0:T(8,128)} %copy-done.1, pred[1024,1024]{1,0:T(32,128)(4,1)} %copy-done.3, pred[]{:T(512)S(6)} %gt.3, f32[1024]{0:T(1024)S(1)} %get-tuple-element.18, ...), kind=kLoop, calls=%fused_computation.25 | loop fusion | flops 16777216 | bytes 26226688 | tf_op jit(solution)/shard_map/convert_element_type | solution.py:58
  154.3 12.0 %multiply_convert_fusion.2 = (bf16[1024,2048]{1,0:T(8,128)(2,1)}, bf16[1024,2048]{1,0:T(8,128)(2,1)}, bf16[1024,2048]{1,0:T(8,128)(2,1)}, bf16[1024,2048]{1,0:T(8,128)(2,1)}) fusion(f32[1024]{0:T(1024)S(1)} %select_reduce_fusion, f32[1024]{0:T(1024)S(1)} %log_add_fusion.2, f32[1024,2048]{1,0:T(8,128)S(1)} %bitcast.92, pred[1024,1024]{1,0:T(32,128)(4,1)} %copy-done.3, ...), kind=kLoop, calls=%fused_computation.26 | loop fusion | flops 33554432 | bytes 51400704 | tf_op jit(solution)/shard_map/convert_element_type | solution.py:58
  166.3 2.5 fusion.47
  180.5 4.2 all-to-all-start.4
  184.7 2.5 fusion.38
  191.4 21.0 %collective-permute-done.2 = f32[1024,384]{1,0:T(8,128)} collective-permute-done((f32[1024,384]{1,0:T(8,128)}, f32[1024,384]{1,0:T(8,128)}, u32[]{:S(2)}, u32[]{:S(2)}) %collective-permute-start.2) | collective-permute-done | bytes 1572896 | tf_op jit(solution)/shard_map/ppermute | solution.py:14
  212.4 2.5 fusion.36
  214.9 8.2 all-to-all-done.4
  223.0 4.2 all-to-all-start.5
  229.6 11.1 %all-to-all-done.5 = bf16[8,128,384]{2,1,0:T(8,128)(2,1)} async-done(((bf16[8,128,384]{2,1,0:T(8,128)(2,1)}), bf16[8,128,384]{2,1,0:T(8,128)(2,1)}, u32[]{:S(2)}, u32[]{:S(2)}) %all-to-all-start.5) | async-done | bytes 786464 | tf_op jit(solution)/shard_map/all_to_all | solution.py:144
  259.9 29.3 %collective-permute-done.3 = f32[1024,384]{0,1:T(8,128)} collective-permute-done((f32[1024,384]{0,1:T(8,128)}, f32[1024,384]{0,1:T(8,128)}, u32[]{:S(2)}, u32[]{:S(2)}) %collective-permute-start.3) | collective-permute-done | bytes 1572896 | tf_op jit(solution)/shard_map/ppermute | solution.py:14
  289.3 2.6 copy_bitcast_fusion
  291.8 4.9 all-to-all-start.6
  301.7 627.7 %all-gather.4.cloned.1.call-done = f32[128,2,3072]{2,1,0:T(2,128)} async-done(((f32[1,2,3072]{2,1,0:T(2,128)}), f32[128,2,3072]{2,1,0:T(2,128)}) %all-gather.4.cloned.1.call-update) | async-done | bytes 3145744 | tf_op jit(solution)/shard_map/all_gather | solution.py:154
  929.4 2.8 reduce_sum.139
  936.3 7.3 reduce-scatter.4.cloned.1.call-done
  (133 shorter events, 73.0 us)
Async XLA Ops:
  7.2 9.6 %copy-start.15 = (bf16[1,128,3072]{2,1,0:T(8,128)(2,1)S(1)}, bf16[1,128,3072]{2,1,0:T(8,128)(2,1)}, u32[]{:S(2)}) copy-start(bf16[1,128,3072]{2,1,0:T(8,128)(2,1)} %param.8) | copy-start | bytes 2359300
  9.5 20.3 %copy-start.26 = (bf16[1,128,3072]{2,1,0:T(8,128)(2,1)S(1)}, bf16[1,128,3072]{2,1,0:T(8,128)(2,1)}, u32[]{:S(2)}) copy-start(bf16[1,128,3072]{2,1,0:T(8,128)(2,1)} %param.10) | copy-start | bytes 2359300
  9.5 16.7 %all-to-all-start.2 = ((bf16[128,8,384]{0,2,1:T(8,128)(2,1)}), bf16[128,8,384]{0,2,1:T(8,128)(2,1)S(1)}, u32[]{:S(2)}, u32[]{:S(2)}) async-start(bf16[128,8,384]{0,2,1:T(8,128)(2,1)} %bitcast.7), calls=%async_computation.2 | async-start | bytes 1572864 | tf_op jit(solution)/shard_map/all_to_all | solution.py:80
  16.8 29.4 %copy-start.13 = (bf16[1,128,3072]{2,1,0:T(8,128)(2,1)S(1)}, bf16[1,128,3072]{2,1,0:T(8,128)(2,1)}, u32[]{:S(2)}) copy-start(bf16[1,128,3072]{2,1,0:T(8,128)(2,1)} %param.7) | copy-start | bytes 2359300
  26.2 26.5 %copy-start.25 = (bf16[128,8,384]{0,2,1:T(8,128)(2,1)}, bf16[128,8,384]{0,2,1:T(8,128)(2,1)S(1)}, u32[]{:S(2)}) copy-start(bf16[128,8,384]{0,2,1:T(8,128)(2,1)S(1)} %all-to-all-done.2) | copy-start | bytes 2359300
  26.3 15.6 %all-to-all-start.1 = ((bf16[128,8,384]{2,0,1:T(8,128)(2,1)}), bf16[128,8,384]{2,0,1:T(8,128)(2,1)S(1)}, u32[]{:S(2)}, u32[]{:S(2)}) async-start(bf16[128,8,384]{2,0,1:T(8,128)(2,1)} %multiply_convert_fusion.5), calls=%async_computation.1 | async-start | bytes 1572864 | tf_op jit(solution)/shard_map/all_to_all | solution.py:79
  41.8 48.7 %copy-start.4 = (bf16[128,8,384]{2,0,1:T(8,128)(2,1)}, bf16[128,8,384]{2,0,1:T(8,128)(2,1)S(1)}, u32[]{:S(2)}) copy-start(bf16[128,8,384]{2,0,1:T(8,128)(2,1)S(1)} %all-to-all-done.1) | copy-start | bytes 2359300
  41.8 22.9 %copy-start.28 = (s32[1,32]{1,0:T(1,128)S(1)}, s32[1,32]{1,0:T(1,128)}, u32[]{:S(2)}) copy-start(s32[1,32]{1,0:T(1,128)} %param.13) | copy-start | bytes 388
  41.8 22.9 %copy-start.27 = (s32[1,1024]{1,0:T(1,128)S(1)}, s32[1,1024]{1,0:T(1,128)}, u32[]{:S(2)}) copy-start(s32[1,1024]{1,0:T(1,128)} %param.12) | copy-start | bytes 12292
  41.8 18.7 %all-to-all-start.3 = ((bf16[128,8,384]{0,2,1:T(8,128)(2,1)}), bf16[128,8,384]{0,2,1:T(8,128)(2,1)}, u32[]{:S(2)}, u32[]{:S(2)}) async-start(bf16[128,8,384]{0,2,1:T(8,128)(2,1)} %bitcast.10), calls=%async_computation.3 | async-start | bytes 1572864 | tf_op jit(solution)/shard_map/all_to_all | solution.py:81
  46.7 39.1 %collective-permute-start = (bf16[1024,384]{1,0:T(8,128)(2,1)S(1)}, bf16[1024,384]{1,0:T(8,128)(2,1)S(1)}, u32[]{:S(2)}, u32[]{:S(2)}) collective-permute-start(bf16[1024,384]{1,0:T(8,128)(2,1)S(1)} %bitcast.93), channel_id=1, source_target_pairs={{0,16},{16,32},{32,48},{48,64},{64,80},{80,96},{96,112},{112,128},... | collective-permute-start | bytes 2359304 | tf_op jit(solution)/shard_map/ppermute | solution.py:14
  60.5 25.3 %all-to-all-start = ((bf16[128,8,384]{2,0,1:T(8,128)(2,1)}), bf16[128,8,384]{2,0,1:T(8,128)(2,1)}, u32[]{:S(2)}, u32[]{:S(2)}) async-start(bf16[128,8,384]{2,0,1:T(8,128)(2,1)} %multiply_convert_fusion.6), calls=%async_computation | async-start | bytes 1572864 | tf_op jit(solution)/shard_map/all_to_all | solution.py:78
  65.5 54.3 %copy-start.3 = (pred[1024,1024]{1,0:T(32,128)(4,1)}, pred[1024,1024]{1,0:T(32,128)(4,1)S(1)}, u32[]{:S(2)}) copy-start(pred[1024,1024]{1,0:T(32,128)(4,1)S(1)} %broadcast_compare_fusion) | copy-start | bytes 3145732
  69.7 39.3 %collective-permute-start.1 = (bf16[1024,384]{1,0:T(8,128)(2,1)S(1)}, bf16[1024,384]{1,0:T(8,128)(2,1)}, u32[]{:S(2)}, u32[]{:S(2)}) collective-permute-start(bf16[1024,384]{1,0:T(8,128)(2,1)S(1)} %bitcast.104), channel_id=1, source_target_pairs={{0,16},{16,32},{32,48},{48,64},{64,80},{80,96},{96,112},{112,128},... | collective-permute-start | bytes 2359304 | tf_op jit(solution)/shard_map/ppermute | solution.py:14
  88.2 12.2 %copy-start = (f32[1024,2048]{1,0:T(8,128)}, f32[1024,2048]{1,0:T(8,128)S(1)}, u32[]{:S(2)}) copy-start(f32[1024,2048]{1,0:T(8,128)S(1)} %fusion.75) | copy-start | bytes 25165828
  90.6 9.8 %copy-start.1 = (f32[1024,2048]{1,0:T(8,128)}, f32[1024,2048]{1,0:T(8,128)S(1)}, u32[]{:S(2)}) copy-start(f32[1024,2048]{1,0:T(8,128)S(1)} %fusion.82) | copy-start | bytes 25165828
  137.9 10.1 %slice-start = ((s8[8388608]{0:T(1024)(128)(4,1)}), s8[4194304]{0:T(1024)(128)(4,1)S(1)}, s32[]{:S(2)}) async-start(s8[8388608]{0:T(1024)(128)(4,1)} %bitcast.89), calls=%async_computation.10 | async-start | bytes 8388608
  137.9 11.6 %slice-start.2 = ((s8[8388608]{0:T(1024)(128)(4,1)}), s8[4194304]{0:T(1024)(128)(4,1)S(1)}, s32[]{:S(2)}) async-start(s8[8388608]{0:T(1024)(128)(4,1)} %bitcast.91), calls=%async_computation.12 | async-start | bytes 8388608
  137.9 12.8 %slice-start.1 = ((s8[8388608]{0:T(1024)(128)(4,1)}), s8[4194304]{0:T(1024)(128)(4,1)S(1)}, s32[]{:S(2)}) async-start(s8[8388608]{0:T(1024)(128)(4,1)} %bitcast.89), calls=%async_computation.11 | async-start | bytes 8388608
  137.9 14.0 %slice-start.3 = ((s8[8388608]{0:T(1024)(128)(4,1)}), s8[4194304]{0:T(1024)(128)(4,1)S(1)}, s32[]{:S(2)}) async-start(s8[8388608]{0:T(1024)(128)(4,1)} %bitcast.91), calls=%async_computation.13 | async-start | bytes 8388608
  137.9 16.4 %copy-start.2 = (f32[2048,1024]{0,1:T(8,128)S(1)}, f32[2048,1024]{0,1:T(8,128)}, u32[]{:S(2)}) copy-start(f32[2048,1024]{0,1:T(8,128)} %fusion.68) | copy-start | bytes 25165828
  174.3 38.1 %collective-permute-start.2 = (f32[1024,384]{1,0:T(8,128)}, f32[1024,384]{1,0:T(8,128)}, u32[]{:S(2)}, u32[]{:S(2)}) collective-permute-start(f32[1024,384]{1,0:T(8,128)} %pad_maximum_fusion), channel_id=1, source_target_pairs={{16,0},{32,16},{48,32},{64,48},{80,64},{96,80},{112,96},{128,112},... | collective-permute-start | bytes 4718600 | tf_op jit(solution)/shard_map/ppermute | solution.py:14
  180.5 42.5 %all-to-all-start.4 = ((bf16[8,128,384]{2,1,0:T(8,128)(2,1)}), bf16[8,128,384]{2,1,0:T(8,128)(2,1)}, u32[]{:S(2)}, u32[]{:S(2)}) async-start(bf16[8,128,384]{2,1,0:T(8,128)(2,1)} %pad_maximum_fusion.2), calls=%async_computation.4 | async-start | bytes 1572864 | tf_op jit(solution)/shard_map/all_to_all | solution.py:141
  189.6 38.0 %copy-start.10 = (f32[16,8,8,384]{3,2,1,0:T(8,128)S(1)}, f32[16,8,8,384]{3,2,1,0:T(8,128)}, u32[]{:S(2)}) copy-start(f32[16,8,8,384]{3,2,1,0:T(8,128)} %copy-done.9) | copy-start | bytes 4718596
  191.4 49.3 %copy-start.8 = (f32[16,8,8,384]{3,2,1,0:T(8,128)S(1)}, f32[16,8,8,384]{3,2,1,0:T(8,128)}, u32[]{:S(2)}) copy-start(f32[16,8,8,384]{3,2,1,0:T(8,128)} %copy-done.7) | copy-start | bytes 4718596
  223.0 17.6 %all-to-all-start.5 = ((bf16[8,128,384]{2,1,0:T(8,128)(2,1)}), bf16[8,128,384]{2,1,0:T(8,128)(2,1)}, u32[]{:S(2)}, u32[]{:S(2)}) async-start(bf16[8,128,384]{2,1,0:T(8,128)(2,1)} %bitcast.122), calls=%async_computation.5 | async-start | bytes 1572864 | tf_op jit(solution)/shard_map/all_to_all | solution.py:144
  227.3 702.1 %all-gather.4.cloned.1.call-start = ((), (), s32[]{:S(2)}) async-start(), calls=%async_computation.8 | async-start | bytes 3170304 | tf_op jit(solution)/shard_map/all_gather | solution.py:154
  229.6 16.1 %copy-start.24 = (bf16[8,128,384]{2,1,0:T(8,128)(2,1)S(1)}, bf16[8,128,384]{2,1,0:T(8,128)(2,1)}, u32[]{:S(2)}) copy-start(bf16[8,128,384]{2,1,0:T(8,128)(2,1)} %copy.81) | copy-start | bytes 2359300
  249.5 39.8 %collective-permute-start.3 = (f32[1024,384]{0,1:T(8,128)}, f32[1024,384]{0,1:T(8,128)}, u32[]{:S(2)}, u32[]{:S(2)}) collective-permute-start(f32[1024,384]{0,1:T(8,128)} %pad_maximum_fusion.1), channel_id=1, source_target_pairs={{16,0},{32,16},{48,32},{64,48},{80,64},{96,80},{112,96},{128,112},... | collective-permute-start | bytes 4718600 | tf_op jit(solution)/shard_map/ppermute | solution.py:14
  291.8 643.4 %all-to-all-start.6 = ((bf16[8,128,384]{1,2,0:T(8,128)(2,1)}), bf16[8,128,384]{1,2,0:T(8,128)(2,1)S(1)}, u32[]{:S(2)}, u32[]{:S(2)}) async-start(bf16[8,128,384]{1,2,0:T(8,128)(2,1)} %copy_bitcast_fusion), calls=%async_computation.6 | async-start | bytes 1572864 | tf_op jit(solution)/shard_map/all_to_all | solution.py:147
  296.7 647.0 %reduce-scatter.4.cloned.1.call-start = ((), (), s32[]{:S(2)}) async-start(), calls=%async_computation.9 | async-start | bytes 2359296
  300.0 633.8 %copy-start.16 = (bf16[1,128,3072]{2,1,0:T(8,128)(2,1)S(1)}, bf16[1,128,3072]{2,1,0:T(8,128)(2,1)}, u32[]{:S(2)}) copy-start(bf16[1,128,3072]{2,1,0:T(8,128)(2,1)} %param.8) | copy-start | bytes 2359300
  (14 other events, 63.1 us)
Sparse Core Ops, SparseCore 0:
  243.5 685.8 all-gather.3
  934.0 9.6 reduce-scatter.3
